TPU v7x, 32 devices: a whole 2x2x4 slice. The times are simulated.
32 devices in a mesh: space: 8 (over z, core), tm: 4 (over y, x).
Axes of the slice: x: 2, y: 2, z: 4, core: 2. Of those that a mesh axis runs over, the one named last changes fastest.
Arguments:
- snapshots: bfloat16 [32768, 512], P('space', 'tm'), may hold values from -6 to 6
- stencil_starts: int32 [512], P('tm'), may hold values from 0 to 508, as said below
- stencil_widths: int32 [512], P('tm'), may hold values from 4 to 40, as said below
- stencil_coeffs: bfloat16 [512, 40], P('tm'), may hold values from -2 to 2
- panels: bfloat16 [512, 256], P('tm'), may hold values from -0.25 to 0.25
Outputs:
- gram: float32 [512, 512], P(('tm', 'space'))
- modes: bfloat16 [32768, 256], P(('space', 'tm'))
Inputs may be any that keep to these rules, and one draw needn't show every extreme that they name: `stencil_starts`: uniform time u's stencil starts inside its own time block, snapshots from (u // 128) * 128 to that plus 128 - 1, and ends before snapshot 512. `stencil_widths`: some stencil has width 40 and some has width 4.
All inputs are finite; a program needn't handle non-finite values.
Results may differ from a plain program's by a relative error of at most 0.0049.
Values may be sent and summed in bfloat16 or wider, within the bound.
A program may use at most 64 MiB of HBM per device.

v0:
```python
import functools

import jax
import jax.numpy as jnp
from jax import lax
from jax.experimental import pallas as pl
from jax.experimental.pallas import tpu as pltpu
from jax.sharding import PartitionSpec as P

F32 = jnp.float32
BF16 = jnp.bfloat16
CORES = 2
CHUNKS = 8


def shifted(value, axis, steps):
    count = lax.axis_size(axis)
    initial, last = (max(0, -steps), min(count, count - steps))
    return lax.ppermute(value, axis, [(source, source + steps) for source in range(initial, last)])


def on_device(snapshots, stencil_starts, stencil_widths, stencil_coeffs, panels):
    rows, block = snapshots.shape
    width_max = stencil_coeffs.shape[1]
    rim = shifted(snapshots[:, : width_max - 1], "tm", -1)
    extended = jnp.concatenate([snapshots, rim], axis=1)
    offsets = stencil_starts - lax.axis_index("tm") * block
    position = jnp.arange(block + width_max - 1, dtype=jnp.int32)[:, None]
    relative = position - offsets[None, :]
    steps = jnp.arange(width_max, dtype=jnp.int32)[:, None, None]
    picked = (relative[None, :, :] == steps) & (steps < stencil_widths[None, None, :])
    coeff_table = stencil_coeffs.T[:, None, :].astype(F32)
    weights = jnp.sum(jnp.where(picked, coeff_table, 0.0), axis=0).astype(BF16)
    resampled = jnp.dot(extended, weights, preferred_element_type=F32).astype(BF16)
    scale = 1.0 / (rows * lax.axis_size("space"))
    share = rows // lax.axis_size("tm")
    whole = lax.all_gather(resampled, "tm", axis=1, tiled=True)
    partial_value = lax.dot_general(
        resampled, whole, (((0,), (0,)), ((), ())), preferred_element_type=F32
    )
    every_panel = lax.all_gather(panels, "tm", axis=0, tiled=True)
    mine = lax.dynamic_slice_in_dim(whole, lax.axis_index("tm") * share, share, 0)
    modes = jnp.dot(mine, every_panel, preferred_element_type=F32).astype(BF16)
    partial_value = partial_value * scale
    gram = lax.psum_scatter(partial_value, "space", scatter_dimension=0, tiled=True)
    return (gram, modes)


def spread(packed, width_max, block):
    table = packed.astype(F32)
    rows = table.shape[0]
    moved = table[width_max : width_max + 1, :].astype(jnp.int32)
    index = lax.broadcasted_iota(jnp.int32, table.shape, 0)
    value = jnp.where(index < width_max, table, 0.0)
    step = 1
    while step < block:
        chosen = (moved & step) != 0
        if step < 8:
            other = pltpu.roll(value, step, 0)
        else:
            empty = jnp.zeros((step, block), F32)
            other = jnp.concatenate([empty, value], axis=0)
            value = jnp.concatenate([value, empty], axis=0)
        value = jnp.where(jnp.broadcast_to(chosen, value.shape), other, value)
        step *= 2
    return value


def kernel(
    nsp, ntm, chunks, halves, width_max,
    snap, starts_in, widths_in, coeffs_in, panels,
    gram_out, modes_out,
    starts, widths, coeffs,
    packed, weights, gathered, resampled, acc, pair_in, mine32, tm_out, tm_in, z_out, z_in, panel_all,
    local_sem, pack_send, pack_recv, row_send, row_recv, panel_send, panel_recv, relay_send, relay_recv, hand_send, hand_recv,
    pair_send, pair_recv, tm_send, tm_recv, z_send, z_recv,
):
    space = lax.axis_index("space")
    t = lax.axis_index("tm")
    zz, core = space // CORES, space % CORES
    nz = nsp // CORES
    block = snap.shape[1]
    share = snap.shape[0] // ntm
    piece = share // chunks
    nu = block * ntm
    wide = nu // halves

    def at(space_id, tm_id):
        return dict(device_id=(space_id, tm_id), device_id_type=pl.DeviceIdType.MESH)

    tm_peers = [t ^ mask for mask in range(ntm - 1, 0, -1)]
    z_peers = [lax.rem(zz + d, nz) * CORES + core for d in range(1, nz)]
    partner = zz * CORES + (1 - core)

    half = block // CORES

    def share_of(tm_id, core_id=core):
        return pl.ds(pl.multiple_of(tm_id * block + core_id * half, half), half)

    def table_of(tm_id, core_id=core):
        rows = packed.shape[1] // CORES
        return packed.at[tm_id, pl.ds(pl.multiple_of(core_id * rows, rows), rows), :]

    barrier = pltpu.get_barrier_semaphore()
    for peer in z_peers:
        pl.semaphore_signal(barrier, inc=1, **at(peer, t))
    for peer in tm_peers:
        pl.semaphore_signal(barrier, inc=1, **at(space, peer))
    pl.semaphore_signal(barrier, inc=1, **at(partner, t))

    columns = pl.ds(pl.multiple_of(t * block, block), block)
    small = [
        pltpu.make_async_copy(source, target, local_sem.at[i])
        for i, (source, target) in enumerate(
            [(starts_in, starts), (widths_in, widths), (coeffs_in, coeffs)]
        )
    ]
    own_rows = pltpu.make_async_copy(
        snap.at[pl.ds(pl.multiple_of(t * share, share), share), :], gathered.at[:, columns], local_sem.at[3]
    )
    own_panels = pltpu.make_async_copy(panels, panel_all.at[columns, :], local_sem.at[4])
    for copy in small:
        copy.start()
    own_rows.start()
    own_panels.start()

    for copy in small:
        copy.wait()
    prow = packed.shape[1]
    turned = jnp.concatenate(
        [coeffs[...].astype(F32), jnp.zeros((prow - width_max, block), F32)], axis=0
    )
    index = lax.broadcasted_iota(jnp.int32, turned.shape, 0)
    offset = (starts[...] - t * block).astype(F32)
    table = jnp.where(index < jnp.broadcast_to(widths[...], turned.shape), turned, 0.0)
    table = jnp.where(index == width_max, jnp.broadcast_to(offset, turned.shape), table)
    packed[t] = table.astype(BF16)

    pl.semaphore_wait(barrier, len(z_peers) + len(tm_peers) + 1)

    sends = []

    def send(src, dst, send_sem, recv_sem, space_id, tm_id):
        copy = pltpu.make_async_remote_copy(
            src_ref=src, dst_ref=dst, send_sem=send_sem, recv_sem=recv_sem, **at(space_id, tm_id))
        copy.start()
        sends.append(copy)

    for i, peer in enumerate(tm_peers):
        send(table_of(t), table_of(t), pack_send.at[i], pack_recv.at[i], space, peer)
    for c in range(chunks):
        for i, peer in enumerate(tm_peers):
            send(
                snap.at[pl.ds(pl.multiple_of(peer * share + c * piece, piece), piece), :],
                gathered.at[pl.ds(c * piece, piece), columns],
                row_send.at[c, i], row_recv.at[c, i], space, peer)
    for i, peer in enumerate(tm_peers):
        send(
            panels.at[pl.ds(pl.multiple_of(core * half, half), half), :], panel_all.at[share_of(t), :],
            panel_send.at[i], panel_recv.at[i], space, peer)

    weights[...] = jnp.zeros_like(weights)
    acc[...] = jnp.zeros_like(acc)

    def arrived(dst, sem):
        pltpu.make_async_remote_copy(
            src_ref=dst, dst_ref=dst, send_sem=sem, recv_sem=sem, **at(space, tm_peers[0])
        ).wait_recv()

    for i, origin in enumerate(tm_peers):
        arrived(table_of(origin), pack_recv.at[i])
        send(table_of(origin), table_of(origin), hand_send.at[i], hand_recv.at[i], partner, t)
    for i, origin in enumerate(tm_peers):
        arrived(table_of(origin, 1 - core), hand_recv.at[i])
    for b in range(ntm):
        value = spread(packed[b], width_max, block).astype(BF16)
        height = min(value.shape[0], nu - b * block)
        weights[b * block : b * block + height, b * block : (b + 1) * block] = value[:height]

    own_rows.wait()
    span = CORES * block

    def resample(c):
        at_rows = pl.ds(pl.multiple_of(c * piece, piece), piece)
        for i, origin in enumerate(tm_peers):
            arrived(
                gathered.at[at_rows, pl.ds(pl.multiple_of(origin * block, block), block)], row_recv.at[c, i]
            )
        for first in range(0, nu, span):
            last = min(first + 2 * span, nu)
            part = jnp.dot(
                gathered[at_rows, first:last], weights[first:last, first : first + span],
                preferred_element_type=F32,
            )
            resampled[at_rows, first : first + span] = part.astype(BF16)
        return resampled[at_rows, :]

    def product(left, right):
        value = lax.dot_general(left, right, (((0,), (0,)), ((), ())), preferred_element_type=F32)
        return value.reshape(acc.shape[:3] + (right.shape[1],))

    def chunk_step(c, carry):
        rows = resample(c)
        acc[...] += product(rows, rows)
        return carry

    lax.fori_loop(0, chunks - 1, chunk_step, 0)
    parts = [slice(h * wide, (h + 1) * wide) for h in range(halves)]
    rows = resample(chunks - 1)
    for h, part in enumerate(parts):
        acc[:, :, :, part] += product(rows, rows[:, part])
        send(acc.at[:, 1 - core, :, part], pair_in.at[:, :, part], pair_send.at[h], pair_recv.at[h], partner, t)

    for h, part in enumerate(parts):
        arrived(pair_in.at[:, :, part], pair_recv.at[h])
        summed = acc[:, pl.ds(core, 1), :, part].reshape(pair_in.shape[:2] + (wide,)) + pair_in[:, :, part]
        summed = summed.reshape(mine32.shape[:3] + (wide,))
        mine32[:, :, :, part] = summed
        tm_out[:, :, :, part] = summed.astype(BF16)
        for i, peer in enumerate(tm_peers):
            send(
                tm_out.at[peer, :, :, part], tm_in.at[i, :, :, part],
                tm_send.at[h, i], tm_recv.at[h, i], space, peer)

    for i, origin in enumerate(tm_peers):
        arrived(panel_all.at[share_of(origin), :], panel_recv.at[i])
        send(
            panel_all.at[share_of(origin), :], panel_all.at[share_of(origin), :],
            relay_send.at[i], relay_recv.at[i], partner, t)

    for h, part in enumerate(parts):
        total = mine32[pl.ds(t, 1), :, :, part].reshape(z_out.shape[:2] + (wide,))
        for i in range(ntm - 1):
            arrived(tm_in.at[i, :, :, part], tm_recv.at[h, i])
            total = total + tm_in[i, :, :, part].astype(F32)
        mine32[pl.ds(t, 1), :, :, part] = total[None]
        z_out[:, :, part] = total.astype(BF16)
        for i, peer in enumerate(z_peers):
            send(
                z_out.at[lax.rem(zz + i + 1, nz), :, part], z_in.at[i, :, part],
                z_send.at[h, i], z_recv.at[h, i], peer, t)
    own_panels.wait()
    for i, origin in enumerate(tm_peers):
        arrived(panel_all.at[share_of(origin, 1 - core), :], relay_recv.at[i])

    def modes_step(c, carry):
        at_rows = pl.ds(pl.multiple_of(c * piece, piece), piece)
        modes_out[at_rows, :] = jnp.dot(
            resampled[at_rows, :], panel_all[...], preferred_element_type=F32).astype(BF16)
        return carry

    lax.fori_loop(0, chunks, modes_step, 0)

    for h, part in enumerate(parts):
        final = mine32[pl.ds(t, 1), pl.ds(zz, 1), :, part].reshape(gram_out.shape[0], wide)
        for i in range(nz - 1):
            arrived(z_in.at[i, :, part], z_recv.at[h, i])
            final = final + z_in[i, :, part].astype(F32)
        gram_out[:, part] = final * (1.0 / (snap.shape[0] * nsp))

    for copy in sends:
        copy.wait_send()


def fused(nsp, ntm, snapshots, stencil_starts, stencil_widths, stencil_coeffs, panels):
    rows, block = snapshots.shape
    width_max = stencil_coeffs.shape[1]
    nmode = panels.shape[1]
    nu, share, nz = block * ntm, rows // ntm, nsp // CORES
    own = nu // (ntm * nsp)
    chunks, halves = CHUNKS, 2
    prow = -(-(width_max + 1) // 32) * 32
    vmem = pl.BlockSpec(memory_space=pltpu.VMEM)
    hbm = pl.BlockSpec(memory_space=pltpu.HBM)
    dma = pltpu.SemaphoreType.DMA
    call = pl.pallas_call(
        functools.partial(kernel, nsp, ntm, chunks, halves, width_max),
        out_shape=(
            jax.ShapeDtypeStruct((own, nu), F32),
            jax.ShapeDtypeStruct((share, nmode), BF16),
        ),
        in_specs=[hbm, hbm, hbm, hbm, hbm],
        out_specs=(vmem, vmem),
        scratch_shapes=[
            pltpu.VMEM((1, block), jnp.int32),
            pltpu.VMEM((1, block), jnp.int32),
            pltpu.VMEM((width_max, block), BF16),
            pltpu.VMEM((ntm, prow, block), BF16),
            pltpu.VMEM((nu, nu), BF16),
            pltpu.VMEM((share, nu), BF16),
            pltpu.VMEM((share, nu), BF16),
            pltpu.VMEM((ntm * nz, CORES, own, nu), F32),
            pltpu.VMEM((ntm * nz, own, nu), F32),
            pltpu.VMEM((ntm, nz, own, nu), F32),
            pltpu.VMEM((ntm, nz, own, nu), BF16),
            pltpu.VMEM((ntm - 1, nz, own, nu), BF16),
            pltpu.VMEM((nz, own, nu), BF16),
            pltpu.VMEM((nz - 1, own, nu), BF16),
            pltpu.VMEM((nu, nmode), BF16),
            dma((5,)),
            dma((ntm - 1,)),
            dma((ntm - 1,)),
            dma((chunks, ntm - 1)),
            dma((chunks, ntm - 1)),
            dma((ntm - 1,)),
            dma((ntm - 1,)),
            dma((ntm - 1,)),
            dma((ntm - 1,)),
            dma((ntm - 1,)),
            dma((ntm - 1,)),
            dma((halves,)),
            dma((halves,)),
            dma((halves, ntm - 1)),
            dma((halves, ntm - 1)),
            dma((halves, nz - 1)),
            dma((halves, nz - 1)),
        ],
        compiler_params=pltpu.CompilerParams(
            collective_id=0, has_side_effects=True, vmem_limit_bytes=48 * 1024 * 1024
        ),
    )
    operands = (
        snapshots, stencil_starts.reshape(1, block), stencil_widths.reshape(1, block), stencil_coeffs.T, panels
    )
    values = call(*(pltpu.with_memory_space_constraint(operand, pltpu.HBM) for operand in operands))
    return pl.pallas_call(
        store,
        out_shape=tuple(jax.ShapeDtypeStruct(value.shape, value.dtype) for value in values),
        in_specs=[vmem, vmem],
        out_specs=(hbm, hbm),
        scratch_shapes=[dma((2,))],
    )(*(pltpu.with_memory_space_constraint(value, pltpu.VMEM) for value in values))


def store(gram, modes, gram_out, modes_out, sem):
    copies = [
        pltpu.make_async_copy(modes, modes_out, sem.at[0]),
        pltpu.make_async_copy(gram, gram_out, sem.at[1]),
    ]
    for copy in copies:
        copy.start()
    for copy in copies:
        copy.wait()


def solution(mesh):
    nsp, ntm = mesh.shape["space"], mesh.shape["tm"]

    def body(snapshots, stencil_starts, stencil_widths, stencil_coeffs, panels):
        rows, block = snapshots.shape
        own = block // nsp
        fits = block == 128 and own % 16 == 0 and nsp % CORES == 0 and ntm % 2 == 0 and ntm & (ntm - 1) == 0 and rows % (64 * ntm) == 0
        if fits and 4 * (block * ntm) ** 2 <= 4 * 1024 * 1024:
            return fused(nsp, ntm, snapshots, stencil_starts, stencil_widths, stencil_coeffs, panels)
        return on_device(snapshots, stencil_starts, stencil_widths, stencil_coeffs, panels)

    return jax.shard_map(
        body,
        mesh=mesh,
        in_specs=(P("space", "tm"), P("tm"), P("tm"), P("tm", None), P("tm", None)),
        out_specs=(P(("tm", "space"), None), P(("space", "tm"), None)),
        check_vma=False,
    )
```

profile of v0, /device:TPU:0, one launch (start us, length us, event | category | flops | bytes accessed | tf_op | source)
XLA Modules:
  0.0 30.7 jit_solution(16225068616583139325)
XLA Ops:
  0.6 29.2 %shard_map.68 = (f32[16,512]{1,0:T(8,128)S(1)}, bf16[1024,256]{1,0:T(8,128)(2,1)S(1)}) custom-call(bf16[4096,128]{1,0:T(8,128)(2,1)} %snap.1, s32[1,128]{1,0:T(1,128)} %bitcast.4, s32[1,128]{1,0:T(1,128)} %bitcast.5, bf16[40,128]{1,0:T(8,128)(2,1)} %bitcast.3, bf16[128,256]{1,0:T(8,128)(2,1)} %panels.1), custom_call_target="tpu_custom_call" | custom-call | tf_op jit(solution)/shard_map/pallas_call | solution.py:325
  29.8 0.8 %shard_map.69 = (f32[16,512]{1,0:T(8,128)}, bf16[1024,256]{1,0:T(8,128)(2,1)}) custom-call(f32[16,512]{1,0:T(8,128)S(1)} %get-tuple-element.4.gram, bf16[1024,256]{1,0:T(8,128)(2,1)S(1)} %get-tuple-element.5.modes), custom_call_target="tpu_custom_call" | custom-call | tf_op jit(solution)/shard_map/pallas_call | solution.py:326
where the time goes:
time: 30.8 us; the launch traced here: 30.7 us
  Pallas kernels  30 us (97%)
  between operations  0.64 us (2%)
    pallas_call x1, Pallas kernels, fused(): call(*(pltpu.with_memory_space_constraint(operand, pltpu.HBM) for operand...  29.2 us
    pallas_call x1, Pallas kernels, fused(): pl.pallas_call(store, out_shape=tuple((jax.ShapeDtypeStruct(value.shape,...  0.81 us

commit v1 on v0

v1 whole, which is shorter than its diff:
```python
import functools

import jax
import jax.numpy as jnp
from jax import lax
from jax.experimental import pallas as pl
from jax.experimental.pallas import tpu as pltpu
from jax.sharding import PartitionSpec as P

F32 = jnp.float32
BF16 = jnp.bfloat16
CORES = 2
CHUNKS = 8


def shifted(value, axis, steps):
    count = lax.axis_size(axis)
    initial, last = (max(0, -steps), min(count, count - steps))
    return lax.ppermute(value, axis, [(source, source + steps) for source in range(initial, last)])


def on_device(snapshots, stencil_starts, stencil_widths, stencil_coeffs, panels):
    rows, block = snapshots.shape
    width_max = stencil_coeffs.shape[1]
    rim = shifted(snapshots[:, : width_max - 1], "tm", -1)
    extended = jnp.concatenate([snapshots, rim], axis=1)
    offsets = stencil_starts - lax.axis_index("tm") * block
    position = jnp.arange(block + width_max - 1, dtype=jnp.int32)[:, None]
    relative = position - offsets[None, :]
    steps = jnp.arange(width_max, dtype=jnp.int32)[:, None, None]
    picked = (relative[None, :, :] == steps) & (steps < stencil_widths[None, None, :])
    coeff_table = stencil_coeffs.T[:, None, :].astype(F32)
    weights = jnp.sum(jnp.where(picked, coeff_table, 0.0), axis=0).astype(BF16)
    resampled = jnp.dot(extended, weights, preferred_element_type=F32).astype(BF16)
    scale = 1.0 / (rows * lax.axis_size("space"))
    share = rows // lax.axis_size("tm")
    whole = lax.all_gather(resampled, "tm", axis=1, tiled=True)
    partial_value = lax.dot_general(
        resampled, whole, (((0,), (0,)), ((), ())), preferred_element_type=F32
    )
    every_panel = lax.all_gather(panels, "tm", axis=0, tiled=True)
    mine = lax.dynamic_slice_in_dim(whole, lax.axis_index("tm") * share, share, 0)
    modes = jnp.dot(mine, every_panel, preferred_element_type=F32).astype(BF16)
    partial_value = partial_value * scale
    gram = lax.psum_scatter(partial_value, "space", scatter_dimension=0, tiled=True)
    return (gram, modes)


def spread(packed, width_max, block):
    table = packed.astype(F32)
    rows = table.shape[0]
    moved = table[width_max : width_max + 1, :].astype(jnp.int32)
    index = lax.broadcasted_iota(jnp.int32, table.shape, 0)
    value = jnp.where(index < width_max, table, 0.0)
    step = 1
    while step < block:
        chosen = (moved & step) != 0
        if step < 8:
            other = pltpu.roll(value, step, 0)
        else:
            empty = jnp.zeros((step, block), F32)
            other = jnp.concatenate([empty, value], axis=0)
            value = jnp.concatenate([value, empty], axis=0)
        value = jnp.where(jnp.broadcast_to(chosen, value.shape), other, value)
        step *= 2
    return value


def kernel(
    nsp, ntm, chunks, halves, width_max,
    snap, starts_in, widths_in, coeffs_in, panels,
    gram_out, modes_out,
    starts, widths, coeffs,
    packed, weights, gathered, both, acc, tm_out, tm_in, z_out, z_in, panel_all,
    local_sem, table_send, table_recv, row_send, row_recv, pass_send, pass_recv,
    panel_send, panel_recv, relay_send, relay_recv, tm_send, tm_recv, z_send, z_recv,
):
    space = lax.axis_index("space")
    t = lax.axis_index("tm")
    zz, core = space // CORES, space % CORES
    nz = nsp // CORES
    nzh = nz // CORES
    block = snap.shape[1]
    share = snap.shape[0] // ntm
    piece = share // chunks
    nu = block * ntm
    wide = nu // halves
    half = block // CORES
    mine = nu // CORES
    own = half // nz
    others = ntm - 1

    def at(space_id, tm_id):
        return dict(device_id=(space_id, tm_id), device_id_type=pl.DeviceIdType.MESH)

    tm_peers = [t ^ mask for mask in range(ntm - 1, 0, -1)]
    partner = zz * CORES + (1 - core)

    def panel_rows(tm_id, core_id):
        return pl.ds(pl.multiple_of(core_id * mine + tm_id * half, half), half)

    barrier = pltpu.get_barrier_semaphore()
    for step in range(1, nsp):
        pl.semaphore_signal(barrier, inc=1, **at(lax.rem(space + step, nsp), t))
    for peer in tm_peers:
        pl.semaphore_signal(barrier, inc=1, **at(space, peer))

    columns = pl.ds(pl.multiple_of(t * block, block), block)
    small = [
        pltpu.make_async_copy(source, target, local_sem.at[i])
        for i, (source, target) in enumerate(
            [(starts_in, starts), (widths_in, widths), (coeffs_in, coeffs)]
        )
    ]
    own_rows = pltpu.make_async_copy(
        snap.at[pl.ds(pl.multiple_of(t * share, share), share), :], gathered.at[:, columns], local_sem.at[3]
    )
    own_panels = [
        pltpu.make_async_copy(panels.at[pl.ds(c * half, half), :], panel_all.at[panel_rows(t, c), :], local_sem.at[4 + c])
        for c in range(CORES)
    ]
    for copy in small:
        copy.start()
    own_rows.start()
    for copy in own_panels:
        copy.start()

    def send(src, dst, send_sem, recv_sem, space_id, tm_id):
        pltpu.make_async_remote_copy(
            src_ref=src, dst_ref=dst, send_sem=send_sem, recv_sem=recv_sem, **at(space_id, tm_id)).start()

    def wait_bytes(ref, sem):
        pltpu.make_async_copy(ref, ref, sem).wait()

    def send_rows(c):
        for peer in tm_peers:
            send(
                snap.at[pl.ds(pl.multiple_of(peer * share + c * piece, piece), piece), :],
                gathered.at[pl.ds(c * piece, piece), columns],
                row_send.at[0], row_recv.at[c], space, peer)

    pl.semaphore_wait(barrier, nsp - 1 + others)

    send_rows(0)

    for copy in small:
        copy.wait()
    prow = packed.shape[1]
    turned = jnp.concatenate(
        [coeffs[...].astype(F32), jnp.zeros((prow - width_max, block), F32)], axis=0
    )
    index = lax.broadcasted_iota(jnp.int32, turned.shape, 0)
    offset = (starts[...] - t * block).astype(F32)
    table = jnp.where(index < jnp.broadcast_to(widths[...], turned.shape), turned, 0.0)
    table = jnp.where(index == width_max, jnp.broadcast_to(offset, turned.shape), table)
    packed[t] = table.astype(BF16)
    for peer in tm_peers:
        send(packed.at[t], packed.at[t], table_send.at[0], table_recv.at[0], space, peer)

    for c in range(1, chunks):
        send_rows(c)
    for peer in tm_peers:
        send(
            panels.at[pl.ds(pl.multiple_of(core * half, half), half), :], panel_all.at[panel_rows(t, core), :],
            panel_send.at[0], panel_recv.at[0], space, peer)

    weights[...] = jnp.zeros_like(weights)
    acc[...] = jnp.zeros_like(acc)

    wait_bytes(packed.at[pl.ds(0, others)], table_recv.at[0])
    span = CORES * block
    for j in range(nu // span):
        left = spread(packed[2 * j], width_max, block)
        right = spread(packed[2 * j + 1], width_max, block)
        height = -(-(left.shape[0] + block) // 16) * 16
        left = jnp.concatenate([left, jnp.zeros((height - left.shape[0], block), F32)], axis=0)
        fill = jnp.zeros((height - block - right.shape[0], block), F32)
        right = jnp.concatenate([jnp.zeros((block, block), F32), right, fill], axis=0)
        low = lax.broadcasted_iota(jnp.int32, left.shape, 1) < half
        first, second = jnp.where(low, left, pltpu.roll(right, half, 1)), jnp.where(low, pltpu.roll(left, half, 1), right)
        height = min(height, nu - j * span)
        at_rows = slice(j * span, j * span + height)
        weights[at_rows, j * span : j * span + block] = first[:height].astype(BF16)
        weights[at_rows, j * span + block : (j + 1) * span] = second[:height].astype(BF16)

    own_rows.wait()

    def resample(c):
        at_rows = pl.ds(pl.multiple_of(c * piece, piece), piece)
        wait_bytes(gathered.at[at_rows, pl.ds(0, others * block)], row_recv.at[c])
        for j in range(nu // span):
            first = j * span
            last = min(first + span + block, nu)
            part = jnp.dot(
                gathered[at_rows, first:last], weights[first:last, first : first + span],
                preferred_element_type=F32,
            ).astype(BF16)
            both[c, core, :, j * block : (j + 1) * block] = part[:, :block]
            both[c, core, :, mine + j * block : mine + (j + 1) * block] = part[:, block:]
        send(both.at[c, core], both.at[c, core], pass_send.at[0], pass_recv.at[c], partner, t)

    def product(c, part):
        left = both[c, :, :, pl.ds(pl.multiple_of(core * mine, mine), mine)].reshape(CORES * piece, mine)
        right = both[c, :, :, part].reshape(CORES * piece, -1)
        value = lax.dot_general(left, right, (((0,), (0,)), ((), ())), preferred_element_type=F32)
        return value.reshape(ntm, half, right.shape[1])

    def partner_rows(c):
        wait_bytes(both.at[c, 1 - core], pass_recv.at[c])

    resample(0)

    def chunk_step(c, carry):
        resample(c)
        partner_rows(c - 1)
        acc[...] += product(c - 1, slice(None))
        return carry

    lax.fori_loop(1, chunks, chunk_step, 0)
    parts = [slice(h * wide, (h + 1) * wide) for h in range(halves)]
    partner_rows(chunks - 1)
    for h, part in enumerate(parts):
        total = acc[:, :, part] + product(chunks - 1, part)
        acc[:, :, part] = total
        tm_out[:, :, part] = total.astype(BF16)
        for i, peer in enumerate(tm_peers):
            send(tm_out.at[peer, :, part], tm_in.at[i, :, part], tm_send.at[0], tm_recv.at[h], space, peer)

    wait_bytes(panel_all.at[pl.ds(0, others * half), :], panel_recv.at[0])
    for origin in tm_peers:
        send(
            panel_all.at[panel_rows(origin, core), :], panel_all.at[panel_rows(origin, core), :],
            relay_send.at[0], relay_recv.at[0], partner, t)

    for h, part in enumerate(parts):
        wait_bytes(tm_in.at[:, :, part], tm_recv.at[h])
        total = acc[pl.ds(t, 1), :, part].reshape(half, wide)
        for i in range(others):
            total = total + tm_in[i, :, part].astype(F32)
        z_out[:, :, :, part] = total.astype(BF16).reshape(nzh, CORES, own, wide)
        for dz in range(nzh):
            for cc in range(CORES):
                to_z = core * nzh + dz
                here = (to_z == zz) & (cc == core)
                src, dst = z_out.at[dz, cc, :, part], z_in.at[zz, :, part]

                @pl.when(here)
                def _():
                    pltpu.make_async_copy(src, dst, z_recv.at[h]).start()

                @pl.when(jnp.logical_not(here))
                def _():
                    send(src, dst, z_send.at[0], z_recv.at[h], to_z * CORES + cc, t)

    for copy in own_panels:
        copy.wait()
    wait_bytes(panel_all.at[pl.ds(0, others * half), :], relay_recv.at[0])

    def modes_step(c, carry):
        at_rows = pl.ds(pl.multiple_of(c * piece, piece), piece)
        modes_out[at_rows, :] = jnp.dot(both[c, core], panel_all[...], preferred_element_type=F32).astype(BF16)
        return carry

    lax.fori_loop(0, chunks, modes_step, 0)

    wait_bytes(snap.at[pl.ds(0, others * share), :], row_send.at[0])
    wait_bytes(packed.at[pl.ds(0, others)], table_send.at[0])
    wait_bytes(both.at[:, 0], pass_send.at[0])
    wait_bytes(panel_all.at[pl.ds(0, others * half), :], panel_send.at[0])
    wait_bytes(panel_all.at[pl.ds(0, others * half), :], relay_send.at[0])
    wait_bytes(tm_in, tm_send.at[0])

    sums = []
    for h, part in enumerate(parts):
        wait_bytes(z_in.at[:, :, part], z_recv.at[h])
        final = z_in[0, :, part].astype(F32)
        for i in range(1, nz):
            final = final + z_in[i, :, part].astype(F32)
        sums.append(final * (1.0 / (snap.shape[0] * nsp)))
    final = jnp.concatenate(sums, axis=1)
    low = lax.broadcasted_iota(jnp.int32, (own, block), 1) < half
    for tile in range(ntm):
        at_tile = (tile // 2) * block
        left, right = final[:, at_tile : at_tile + block], final[:, mine + at_tile : mine + at_tile + block]
        if tile % 2:
            left = pltpu.roll(left, half, 1)
        else:
            right = pltpu.roll(right, half, 1)
        gram_out[:, tile * block : (tile + 1) * block] = jnp.where(low, left, right)

    inside = zz // nzh == core

    @pl.when(inside)
    def _():
        wait_bytes(z_in.at[pl.ds(0, nz - 1)], z_send.at[0])

    @pl.when(jnp.logical_not(inside))
    def _():
        wait_bytes(z_in, z_send.at[0])


def fused(nsp, ntm, snapshots, stencil_starts, stencil_widths, stencil_coeffs, panels):
    rows, block = snapshots.shape
    width_max = stencil_coeffs.shape[1]
    nmode = panels.shape[1]
    nu, share, nz = block * ntm, rows // ntm, nsp // CORES
    own, half = nu // (ntm * nsp), block // CORES
    chunks, halves = CHUNKS, 2
    piece = share // chunks
    prow = -(-(width_max + 1) // 16) * 16
    vmem = pl.BlockSpec(memory_space=pltpu.VMEM)
    hbm = pl.BlockSpec(memory_space=pltpu.HBM)
    dma = pltpu.SemaphoreType.DMA
    call = pl.pallas_call(
        functools.partial(kernel, nsp, ntm, chunks, halves, width_max),
        out_shape=(
            jax.ShapeDtypeStruct((own, nu), F32),
            jax.ShapeDtypeStruct((share, nmode), BF16),
        ),
        in_specs=[hbm, hbm, hbm, hbm, hbm],
        out_specs=(vmem, vmem),
        scratch_shapes=[
            pltpu.VMEM((1, block), jnp.int32),
            pltpu.VMEM((1, block), jnp.int32),
            pltpu.VMEM((width_max, block), BF16),
            pltpu.VMEM((ntm, prow, block), BF16),
            pltpu.VMEM((nu, nu), BF16),
            pltpu.VMEM((share, nu), BF16),
            pltpu.VMEM((chunks, CORES, piece, nu), BF16),
            pltpu.VMEM((ntm, half, nu), F32),
            pltpu.VMEM((ntm, half, nu), BF16),
            pltpu.VMEM((ntm - 1, half, nu), BF16),
            pltpu.VMEM((nz // CORES, CORES, own, nu), BF16),
            pltpu.VMEM((nz, own, nu), BF16),
            pltpu.VMEM((nu, nmode), BF16),
            dma((4 + CORES,)),
            dma((1,)),
            dma((1,)),
            dma((1,)),
            dma((chunks,)),
            dma((1,)),
            dma((chunks,)),
            dma((1,)),
            dma((1,)),
            dma((1,)),
            dma((1,)),
            dma((1,)),
            dma((halves,)),
            dma((1,)),
            dma((halves,)),
        ],
        compiler_params=pltpu.CompilerParams(
            collective_id=0, has_side_effects=True, vmem_limit_bytes=48 * 1024 * 1024
        ),
    )
    operands = (
        snapshots, stencil_starts.reshape(1, block), stencil_widths.reshape(1, block), stencil_coeffs.T, panels
    )
    values = call(*(pltpu.with_memory_space_constraint(operand, pltpu.HBM) for operand in operands))
    return pl.pallas_call(
        store,
        out_shape=tuple(jax.ShapeDtypeStruct(value.shape, value.dtype) for value in values),
        in_specs=[vmem, vmem],
        out_specs=(hbm, hbm),
        scratch_shapes=[dma((2,))],
    )(*(pltpu.with_memory_space_constraint(value, pltpu.VMEM) for value in values))


def store(gram, modes, gram_out, modes_out, sem):
    copies = [
        pltpu.make_async_copy(modes, modes_out, sem.at[0]),
        pltpu.make_async_copy(gram, gram_out, sem.at[1]),
    ]
    for copy in copies:
        copy.start()
    for copy in copies:
        copy.wait()


def solution(mesh):
    nsp, ntm = mesh.shape["space"], mesh.shape["tm"]

    def body(snapshots, stencil_starts, stencil_widths, stencil_coeffs, panels):
        rows, block = snapshots.shape
        own = block // nsp
        fits = block == 128 and own % 16 == 0 and nsp % (CORES * CORES) == 0 and ntm % 2 == 0 and ntm & (ntm - 1) == 0 and rows % (64 * ntm) == 0
        if fits and 4 * (block * ntm) ** 2 <= 4 * 1024 * 1024:
            return fused(nsp, ntm, snapshots, stencil_starts, stencil_widths, stencil_coeffs, panels)
        return on_device(snapshots, stencil_starts, stencil_widths, stencil_coeffs, panels)

    return jax.shard_map(
        body,
        mesh=mesh,
        in_specs=(P("space", "tm"), P("tm"), P("tm"), P("tm", None), P("tm", None)),
        out_specs=(P(("tm", "space"), None), P(("space", "tm"), None)),
        check_vma=False,
    )
```

time: 30.8 us -> 31.3 us (1.016)
  Pallas kernels: 30 us -> 30.5 us
    pallas_call x1, Pallas kernels: 29.2 us -> 29.7 us  [fused(): call(*(pltpu.with_memory_space_constraint(operand, pltpu.HBM) for operand...]
where the time goes in v1:
time: 31.3 us; the launch traced here: 31.1 us
  Pallas kernels  30.5 us (97%)
  between operations  0.64 us (2%)
    pallas_call x1, Pallas kernels, fused(): call(*(pltpu.with_memory_space_constraint(operand, pltpu.HBM) for operand...  29.7 us
    pallas_call x1, Pallas kernels, fused(): pl.pallas_call(store, out_shape=tuple((jax.ShapeDtypeStruct(value.shape,...  0.81 us

profile of v1, /device:TPU:0, one launch (start us, length us, event | category | flops | bytes accessed | tf_op | source)
XLA Modules:
  0.0 31.1 jit_solution(11698512226057811332)
XLA Ops:
  0.6 29.7 %shard_map.68 = (f32[16,512]{1,0:T(8,128)S(1)}, bf16[1024,256]{1,0:T(8,128)(2,1)S(1)}) custom-call(bf16[4096,128]{1,0:T(8,128)(2,1)} %snap.1, s32[1,128]{1,0:T(1,128)} %bitcast.4, s32[1,128]{1,0:T(1,128)} %bitcast.5, bf16[40,128]{1,0:T(8,128)(2,1)} %bitcast.3, bf16[128,256]{1,0:T(8,128)(2,1)} %panels.1), custom_call_target="tpu_custom_call" | custom-call | tf_op jit(solution)/shard_map/pallas_call | solution.py:359
  30.3 0.8 %shard_map.69 = (f32[16,512]{1,0:T(8,128)}, bf16[1024,256]{1,0:T(8,128)(2,1)}) custom-call(f32[16,512]{1,0:T(8,128)S(1)} %get-tuple-element.4.gram, bf16[1024,256]{1,0:T(8,128)(2,1)S(1)} %get-tuple-element.5.modes), custom_call_target="tpu_custom_call" | custom-call | tf_op jit(solution)/shard_map/pallas_call | solution.py:360

commit v2 on v1

--- a/solution.py
+++ b/solution.py
@@ -10,7 +10,8 @@
 F32 = jnp.float32
 BF16 = jnp.bfloat16
 CORES = 2
-CHUNKS = 8
+CHUNKS = 4
+EARLY = 1
 
 
 def shifted(value, axis, steps):
@@ -67,13 +68,14 @@
 
 
 def kernel(
-    nsp, ntm, chunks, halves, width_max,
+    nsp, ntm, chunks, width_max,
     snap, starts_in, widths_in, coeffs_in, panels,
     gram_out, modes_out,
     starts, widths, coeffs,
-    packed, weights, gathered, both, acc, tm_out, tm_in, z_out, z_in, panel_all,
-    local_sem, table_send, table_recv, row_send, row_recv, pass_send, pass_recv,
-    panel_send, panel_recv, relay_send, relay_recv, tm_send, tm_recv, z_send, z_recv,
+    packed, weights, gathered, both, acc, tm_out, tm_in, z_out, z_in,
+    first_in, first_sum, first_out, second_in, panel_all,
+    ready, local_sem, table_send, table_recv, row_send, row_recv, pass_send, pass_recv,
+    panel_send, panel_recv, tm_send, tm_recv, z_send, z_recv, mix_send, mix_recv,
 ):
     space = lax.axis_index("space")
     t = lax.axis_index("tm")
@@ -84,7 +86,7 @@
     share = snap.shape[0] // ntm
     piece = share // chunks
     nu = block * ntm
-    wide = nu // halves
+    quarter = nu // 4
     half = block // CORES
     mine = nu // CORES
     own = half // nz
@@ -96,14 +98,23 @@
     tm_peers = [t ^ mask for mask in range(ntm - 1, 0, -1)]
     partner = zz * CORES + (1 - core)
 
-    def panel_rows(tm_id, core_id):
-        return pl.ds(pl.multiple_of(core_id * mine + tm_id * half, half), half)
+    near_peers = [peer for peer, mask in zip(tm_peers, range(ntm - 1, 0, -1)) if mask & (mask - 1) == 0]
+    far_peers = [peer for peer, mask in zip(tm_peers, range(ntm - 1, 0, -1)) if mask & (mask - 1)]
+    above, below = zz + 1 < nz, zz > 0
 
     barrier = pltpu.get_barrier_semaphore()
-    for step in range(1, nsp):
-        pl.semaphore_signal(barrier, inc=1, **at(lax.rem(space + step, nsp), t))
-    for peer in tm_peers:
+    for peer in near_peers:
         pl.semaphore_signal(barrier, inc=1, **at(space, peer))
+
+    @pl.when(above)
+    def _():
+        pl.semaphore_signal(barrier, inc=1, **at(space + CORES, t))
+
+    @pl.when(below)
+    def _():
+        pl.semaphore_signal(barrier, inc=1, **at(space - CORES, t))
+
+    pl.semaphore_signal(barrier, inc=1, **at(partner, t))
 
     columns = pl.ds(pl.multiple_of(t * block, block), block)
     small = [
@@ -115,15 +126,13 @@
     own_rows = pltpu.make_async_copy(
         snap.at[pl.ds(pl.multiple_of(t * share, share), share), :], gathered.at[:, columns], local_sem.at[3]
     )
-    own_panels = [
-        pltpu.make_async_copy(panels.at[pl.ds(c * half, half), :], panel_all.at[panel_rows(t, c), :], local_sem.at[4 + c])
-        for c in range(CORES)
-    ]
+    slot = pl.ds(pl.multiple_of(zz * own, own), own)
+    panel_part = panels.at[pl.ds(pl.multiple_of(core * half + zz * own, own), own), :]
+    own_panels = pltpu.make_async_copy(panel_part, panel_all.at[core, t, slot, :], local_sem.at[4])
     for copy in small:
         copy.start()
     own_rows.start()
-    for copy in own_panels:
-        copy.start()
+    own_panels.start()
 
     def send(src, dst, send_sem, recv_sem, space_id, tm_id):
         pltpu.make_async_remote_copy(
@@ -132,17 +141,17 @@
     def wait_bytes(ref, sem):
         pltpu.make_async_copy(ref, ref, sem).wait()
 
-    def send_rows(c):
-        for peer in tm_peers:
+    def send_rows(c, peers):
+        for peer in peers:
             send(
                 snap.at[pl.ds(pl.multiple_of(peer * share + c * piece, piece), piece), :],
                 gathered.at[pl.ds(c * piece, piece), columns],
                 row_send.at[0], row_recv.at[c], space, peer)
 
-    pl.semaphore_wait(barrier, nsp - 1 + others)
-
-    send_rows(0)
-
+    pl.semaphore_wait(barrier, len(near_peers) + 1 + above.astype(jnp.int32) + below.astype(jnp.int32))
+
+    for peer in near_peers[-1:] if far_peers else []:
+        pl.semaphore_signal(ready.at[0], inc=1, **at(space, peer))
     for copy in small:
         copy.wait()
     prow = packed.shape[1]
@@ -154,18 +163,46 @@
     table = jnp.where(index < jnp.broadcast_to(widths[...], turned.shape), turned, 0.0)
     table = jnp.where(index == width_max, jnp.broadcast_to(offset, turned.shape), table)
     packed[t] = table.astype(BF16)
-    for peer in tm_peers:
-        send(packed.at[t], packed.at[t], table_send.at[0], table_recv.at[0], space, peer)
-
-    for c in range(1, chunks):
-        send_rows(c)
-    for peer in tm_peers:
-        send(
-            panels.at[pl.ds(pl.multiple_of(core * half, half), half), :], panel_all.at[panel_rows(t, core), :],
-            panel_send.at[0], panel_recv.at[0], space, peer)
+
+    def send_table(peers):
+        for peer in peers:
+            send(packed.at[t], packed.at[t], table_send.at[0], table_recv.at[0], space, peer)
+
+    send_table(near_peers)
+    early = min(EARLY, chunks) if far_peers else 0
+    for c in range(early):
+        send_rows(c, near_peers)
+    if far_peers:
+        pl.semaphore_wait(ready.at[0], 1)
+    send_table(far_peers)
+    for c in range(early):
+        send_rows(c, far_peers)
+    for c in range(early, chunks):
+        send_rows(c, tm_peers)
+        if c == early:
+            for peer in tm_peers:
+                send(panel_part, panel_all.at[core, t, slot, :], panel_send.at[0], panel_recv.at[0], space, peer)
 
     weights[...] = jnp.zeros_like(weights)
     acc[...] = jnp.zeros_like(acc)
+
+    line = ((1, zz, nz - 1 - zz, -CORES), (2, nz - 1 - zz, zz, CORES))
+
+    def pass_on(sem, when, toward):
+        @pl.when(when)
+        def _():
+            pl.semaphore_signal(ready.at[sem], inc=1, **at(space + toward, t))
+
+    for sem, ahead, behind, toward in line:
+        pass_on(sem, ahead > 0, toward)
+    for step in range(1, nz):
+        for sem, ahead, behind, toward in line:
+
+            @pl.when(step <= behind)
+            def _():
+                pl.semaphore_wait(ready.at[sem], 1)
+
+            pass_on(sem, (step <= behind) & (ahead > 0), toward)
 
     wait_bytes(packed.at[pl.ds(0, others)], table_recv.at[0])
     span = CORES * block
@@ -208,76 +245,112 @@
     def partner_rows(c):
         wait_bytes(both.at[c, 1 - core], pass_recv.at[c])
 
-    resample(0)
+    lag = 1
+
+    def resample_step(c, carry):
+        resample(c)
+        return carry
+
+    def add_step(c, carry):
+        partner_rows(c)
+        acc[...] += product(c, slice(None))
+        return carry
 
     def chunk_step(c, carry):
         resample(c)
-        partner_rows(c - 1)
-        acc[...] += product(c - 1, slice(None))
-        return carry
-
-    lax.fori_loop(1, chunks, chunk_step, 0)
-    parts = [slice(h * wide, (h + 1) * wide) for h in range(halves)]
+        return add_step(c - lag, carry)
+
+    lax.fori_loop(0, lag, resample_step, 0)
+
+    own_panels.wait()
+    wait_bytes(panel_all.at[core, pl.ds(0, others), slot], panel_recv.at[0])
+    for d in range(1, nz):
+        peer = lax.rem(zz + d, nz) * CORES + core
+        send(panel_all.at[core, :, slot], panel_all.at[core, :, slot], panel_send.at[1], panel_recv.at[1], peer, t)
+    lax.fori_loop(lag, chunks, chunk_step, 0)
+    parts = [slice(nu - 2 * quarter, nu - quarter), slice(0, nu - 2 * quarter)]
+    ahead_part = slice(nu - quarter, nu)
     partner_rows(chunks - 1)
-    for h, part in enumerate(parts):
+    def finish(part):
         total = acc[:, :, part] + product(chunks - 1, part)
         acc[:, :, part] = total
         tm_out[:, :, part] = total.astype(BF16)
+
+    def send_tm(h):
         for i, peer in enumerate(tm_peers):
-            send(tm_out.at[peer, :, part], tm_in.at[i, :, part], tm_send.at[0], tm_recv.at[h], space, peer)
-
-    wait_bytes(panel_all.at[pl.ds(0, others * half), :], panel_recv.at[0])
-    for origin in tm_peers:
-        send(
-            panel_all.at[panel_rows(origin, core), :], panel_all.at[panel_rows(origin, core), :],
-            relay_send.at[0], relay_recv.at[0], partner, t)
-
-    for h, part in enumerate(parts):
-        wait_bytes(tm_in.at[:, :, part], tm_recv.at[h])
-        total = acc[pl.ds(t, 1), :, part].reshape(half, wide)
-        for i in range(others):
-            total = total + tm_in[i, :, part].astype(F32)
-        z_out[:, :, :, part] = total.astype(BF16).reshape(nzh, CORES, own, wide)
+            send(tm_out.at[peer, :, parts[h]], tm_in.at[i, :, parts[h]], tm_send.at[0], tm_recv.at[h], space, peer)
+
+    def send_line(pick, target, send_sem, recv_sem):
         for dz in range(nzh):
             for cc in range(CORES):
                 to_z = core * nzh + dz
                 here = (to_z == zz) & (cc == core)
-                src, dst = z_out.at[dz, cc, :, part], z_in.at[zz, :, part]
+                source = pick(dz * CORES + cc)
 
                 @pl.when(here)
                 def _():
-                    pltpu.make_async_copy(src, dst, z_recv.at[h]).start()
+                    pltpu.make_async_copy(source, target, recv_sem).start()
 
                 @pl.when(jnp.logical_not(here))
                 def _():
-                    send(src, dst, z_send.at[0], z_recv.at[h], to_z * CORES + cc, t)
-
-    for copy in own_panels:
-        copy.wait()
-    wait_bytes(panel_all.at[pl.ds(0, others * half), :], relay_recv.at[0])
-
-    def modes_step(c, carry):
-        at_rows = pl.ds(pl.multiple_of(c * piece, piece), piece)
-        modes_out[at_rows, :] = jnp.dot(both[c, core], panel_all[...], preferred_element_type=F32).astype(BF16)
-        return carry
-
-    lax.fori_loop(0, chunks, modes_step, 0)
+                    send(source, target, send_sem, recv_sem, to_z * CORES + cc, t)
+
+    finish(slice(nu - 2 * quarter, nu))
+    send_line(
+        lambda k: tm_out.at[:, pl.ds(k * own, own), ahead_part], first_in.at[zz], mix_send.at[0], mix_recv.at[0])
+    send_tm(0)
+    finish(parts[1])
+    send_tm(1)
+
+    for h, part in enumerate(parts):
+        wait_bytes(tm_in.at[:, :, part], tm_recv.at[h])
+        total = acc[pl.ds(t, 1), :, part].reshape(half, part.stop - part.start)
+        for i in range(others):
+            total = total + tm_in[i, :, part].astype(F32)
+        z_out[:, :, part] = total.astype(BF16).reshape(nz, own, part.stop - part.start)
+        send_line(lambda k: z_out.at[k, :, part], z_in.at[zz, :, part], z_send.at[0], z_recv.at[h])
+
+    wait_bytes(panel_all.at[core, :, pl.ds(0, half - own)], panel_recv.at[1])
+    send(panel_all.at[core], panel_all.at[core], panel_send.at[2], panel_recv.at[2], partner, t)
+    wait_bytes(first_in, mix_recv.at[0])
+    total = first_in[0].astype(F32)
+    for i in range(1, nz):
+        total = total + first_in[i].astype(F32)
+    first_sum[...] = total
+    first_out[...] = total.astype(BF16)
+    for i, peer in enumerate(tm_peers):
+        send(first_out.at[peer], second_in.at[i], mix_send.at[1], mix_recv.at[1], space, peer)
+    wait_bytes(panel_all.at[1 - core], panel_recv.at[2])
+
+    group = chunks // 2
+    table = panel_all[...].reshape(nu, -1)
+    for c in range(0, chunks, group):
+        rows = both[c : c + group, core].reshape(group * piece, nu)
+        value = jnp.dot(rows, table, preferred_element_type=F32)
+        modes_out[c * piece : (c + group) * piece, :] = value.astype(BF16)
 
     wait_bytes(snap.at[pl.ds(0, others * share), :], row_send.at[0])
     wait_bytes(packed.at[pl.ds(0, others)], table_send.at[0])
     wait_bytes(both.at[:, 0], pass_send.at[0])
-    wait_bytes(panel_all.at[pl.ds(0, others * half), :], panel_send.at[0])
-    wait_bytes(panel_all.at[pl.ds(0, others * half), :], relay_send.at[0])
+    wait_bytes(panel_all.at[core, pl.ds(0, others), slot], panel_send.at[0])
+    wait_bytes(panel_all.at[core, :, pl.ds(0, half - own)], panel_send.at[1])
+    wait_bytes(panel_all.at[core], panel_send.at[2])
     wait_bytes(tm_in, tm_send.at[0])
 
-    sums = []
+    wait_bytes(second_in, mix_send.at[1])
+
+    wait_bytes(second_in, mix_recv.at[1])
+    total = first_sum[pl.ds(t, 1)].reshape(own, quarter)
+    for i in range(others):
+        total = total + second_in[i].astype(F32)
+    sums = [total]
     for h, part in enumerate(parts):
         wait_bytes(z_in.at[:, :, part], z_recv.at[h])
-        final = z_in[0, :, part].astype(F32)
+        total = z_in[0, :, part].astype(F32)
         for i in range(1, nz):
-            final = final + z_in[i, :, part].astype(F32)
-        sums.append(final * (1.0 / (snap.shape[0] * nsp)))
-    final = jnp.concatenate(sums, axis=1)
+            total = total + z_in[i, :, part].astype(F32)
+        sums.insert(0, total)
+    final = jnp.concatenate(sums[:1] + sums[1:], axis=1) * (1.0 / (snap.shape[0] * nsp))
     low = lax.broadcasted_iota(jnp.int32, (own, block), 1) < half
     for tile in range(ntm):
         at_tile = (tile // 2) * block
@@ -293,10 +366,12 @@
     @pl.when(inside)
     def _():
         wait_bytes(z_in.at[pl.ds(0, nz - 1)], z_send.at[0])
+        wait_bytes(first_in.at[pl.ds(0, nz - 1)], mix_send.at[0])
 
     @pl.when(jnp.logical_not(inside))
     def _():
         wait_bytes(z_in, z_send.at[0])
+        wait_bytes(first_in, mix_send.at[0])
 
 
 def fused(nsp, ntm, snapshots, stencil_starts, stencil_widths, stencil_coeffs, panels):
@@ -305,14 +380,14 @@
     nmode = panels.shape[1]
     nu, share, nz = block * ntm, rows // ntm, nsp // CORES
     own, half = nu // (ntm * nsp), block // CORES
-    chunks, halves = CHUNKS, 2
+    chunks, quarter = CHUNKS, nu // 4
     piece = share // chunks
     prow = -(-(width_max + 1) // 16) * 16
     vmem = pl.BlockSpec(memory_space=pltpu.VMEM)
     hbm = pl.BlockSpec(memory_space=pltpu.HBM)
     dma = pltpu.SemaphoreType.DMA
     call = pl.pallas_call(
-        functools.partial(kernel, nsp, ntm, chunks, halves, width_max),
+        functools.partial(kernel, nsp, ntm, chunks, width_max),
         out_shape=(
             jax.ShapeDtypeStruct((own, nu), F32),
             jax.ShapeDtypeStruct((share, nmode), BF16),
@@ -329,25 +404,30 @@
             pltpu.VMEM((chunks, CORES, piece, nu), BF16),
             pltpu.VMEM((ntm, half, nu), F32),
             pltpu.VMEM((ntm, half, nu), BF16),
-            pltpu.VMEM((ntm - 1, half, nu), BF16),
-            pltpu.VMEM((nz // CORES, CORES, own, nu), BF16),
-            pltpu.VMEM((nz, own, nu), BF16),
-            pltpu.VMEM((nu, nmode), BF16),
-            dma((4 + CORES,)),
+            pltpu.VMEM((ntm - 1, half, nu - quarter), BF16),
+            pltpu.VMEM((nz, own, nu - quarter), BF16),
+            pltpu.VMEM((nz, own, nu - quarter), BF16),
+            pltpu.VMEM((nz, ntm, own, quarter), BF16),
+            pltpu.VMEM((ntm, own, quarter), F32),
+            pltpu.VMEM((ntm, own, quarter), BF16),
+            pltpu.VMEM((ntm - 1, own, quarter), BF16),
+            pltpu.VMEM((CORES, ntm, half, nmode), BF16),
+            pltpu.SemaphoreType.REGULAR((3,)),
+            dma((5,)),
             dma((1,)),
             dma((1,)),
             dma((1,)),
             dma((chunks,)),
             dma((1,)),
             dma((chunks,)),
-            dma((1,)),
-            dma((1,)),
-            dma((1,)),
-            dma((1,)),
-            dma((1,)),
-            dma((halves,)),
-            dma((1,)),
-            dma((halves,)),
+            dma((3,)),
+            dma((3,)),
+            dma((1,)),
+            dma((2,)),
+            dma((1,)),
+            dma((2,)),
+            dma((2,)),
+            dma((2,)),
         ],
         compiler_params=pltpu.CompilerParams(
             collective_id=0, has_side_effects=True, vmem_limit_bytes=48 * 1024 * 1024
@@ -383,7 +463,7 @@
     def body(snapshots, stencil_starts, stencil_widths, stencil_coeffs, panels):
         rows, block = snapshots.shape
         own = block // nsp
-        fits = block == 128 and own % 16 == 0 and nsp % (CORES * CORES) == 0 and ntm % 2 == 0 and ntm & (ntm - 1) == 0 and rows % (64 * ntm) == 0
+        fits = block == 128 and own % 16 == 0 and nsp % (CORES * CORES) == 0 and 2 <= ntm <= 4 and ntm & (ntm - 1) == 0 and rows % (64 * ntm) == 0 and block * ntm % 512 == 0
         if fits and 4 * (block * ntm) ** 2 <= 4 * 1024 * 1024:
             return fused(nsp, ntm, snapshots, stencil_starts, stencil_widths, stencil_coeffs, panels)
         return on_device(snapshots, stencil_starts, stencil_widths, stencil_coeffs, panels)

time: 31.3 us -> 29.7 us (0.949)
  Pallas kernels: 30.5 us -> 28.9 us
    pallas_call x1, Pallas kernels: 29.7 us -> 28.1 us  [fused(): call(*(pltpu.with_memory_space_constraint(operand, pltpu.HBM) for operand...]
where the time goes in v2:
time: 29.7 us; the launch traced here: 29.5 us
  Pallas kernels  28.9 us (97%)
  between operations  0.64 us (2%)
    pallas_call x1, Pallas kernels, fused(): call(*(pltpu.with_memory_space_constraint(operand, pltpu.HBM) for operand...  28.1 us
    pallas_call x1, Pallas kernels, fused(): pl.pallas_call(store, out_shape=tuple((jax.ShapeDtypeStruct(value.shape,...  0.81 us

profile of v2, /device:TPU:0, one launch (start us, length us, event | category | flops | bytes accessed | tf_op | source)
XLA Modules:
  0.0 29.5 jit_solution(12184699358786756853)
XLA Ops:
  0.6 28.1 %shard_map.68 = (f32[16,512]{1,0:T(8,128)S(1)}, bf16[1024,256]{1,0:T(8,128)(2,1)S(1)}) custom-call(bf16[4096,128]{1,0:T(8,128)(2,1)} %snap.1, s32[1,128]{1,0:T(1,128)} %bitcast.4, s32[1,128]{1,0:T(1,128)} %bitcast.5, bf16[40,128]{1,0:T(8,128)(2,1)} %bitcast.3, bf16[128,256]{1,0:T(8,128)(2,1)} %panels.1), custom_call_target="tpu_custom_call" | custom-call | tf_op jit(solution)/shard_map/pallas_call | solution.py:439
  28.7 0.8 %shard_map.69 = (f32[16,512]{1,0:T(8,128)}, bf16[1024,256]{1,0:T(8,128)(2,1)}) custom-call(f32[16,512]{1,0:T(8,128)S(1)} %get-tuple-element.4.gram, bf16[1024,256]{1,0:T(8,128)(2,1)S(1)} %get-tuple-element.5.modes), custom_call_target="tpu_custom_call" | custom-call | tf_op jit(solution)/shard_map/pallas_call | solution.py:440

commit v3 on v2

--- a/solution.py
+++ b/solution.py
@@ -10,8 +10,7 @@
 F32 = jnp.float32
 BF16 = jnp.bfloat16
 CORES = 2
-CHUNKS = 4
-EARLY = 1
+SPLIT = (4, 4, 4, 4)
 
 
 def shifted(value, axis, steps):
@@ -68,7 +67,7 @@
 
 
 def kernel(
-    nsp, ntm, chunks, width_max,
+    nsp, ntm, width_max,
     snap, starts_in, widths_in, coeffs_in, panels,
     gram_out, modes_out,
     starts, widths, coeffs,
@@ -84,7 +83,9 @@
     nzh = nz // CORES
     block = snap.shape[1]
     share = snap.shape[0] // ntm
-    piece = share // chunks
+    chunks = len(SPLIT)
+    sizes = [part * share // sum(SPLIT) for part in SPLIT]
+    begins = [sum(sizes[:c]) for c in range(chunks)]
     nu = block * ntm
     quarter = nu // 4
     half = block // CORES
@@ -144,8 +145,8 @@
     def send_rows(c, peers):
         for peer in peers:
             send(
-                snap.at[pl.ds(pl.multiple_of(peer * share + c * piece, piece), piece), :],
-                gathered.at[pl.ds(c * piece, piece), columns],
+                snap.at[pl.ds(pl.multiple_of(peer * share + begins[c], 16), sizes[c]), :],
+                gathered.at[pl.ds(begins[c], sizes[c]), columns],
                 row_send.at[0], row_recv.at[c], space, peer)
 
     pl.semaphore_wait(barrier, len(near_peers) + 1 + above.astype(jnp.int32) + below.astype(jnp.int32))
@@ -169,7 +170,7 @@
             send(packed.at[t], packed.at[t], table_send.at[0], table_recv.at[0], space, peer)
 
     send_table(near_peers)
-    early = min(EARLY, chunks) if far_peers else 0
+    early = 1 if far_peers else 0
     for c in range(early):
         send_rows(c, near_peers)
     if far_peers:
@@ -178,10 +179,10 @@
     for c in range(early):
         send_rows(c, far_peers)
     for c in range(early, chunks):
-        send_rows(c, tm_peers)
         if c == early:
             for peer in tm_peers:
                 send(panel_part, panel_all.at[core, t, slot, :], panel_send.at[0], panel_recv.at[0], space, peer)
+        send_rows(c, tm_peers)
 
     weights[...] = jnp.zeros_like(weights)
     acc[...] = jnp.zeros_like(acc)
@@ -222,8 +223,11 @@
 
     own_rows.wait()
 
+    def rows_of(c, core_id):
+        return pl.ds(pl.multiple_of(CORES * begins[c] + core_id * sizes[c], 16), sizes[c])
+
     def resample(c):
-        at_rows = pl.ds(pl.multiple_of(c * piece, piece), piece)
+        at_rows = slice(begins[c], begins[c] + sizes[c])
         wait_bytes(gathered.at[at_rows, pl.ds(0, others * block)], row_recv.at[c])
         for j in range(nu // span):
             first = j * span
@@ -232,47 +236,67 @@
                 gathered[at_rows, first:last], weights[first:last, first : first + span],
                 preferred_element_type=F32,
             ).astype(BF16)
-            both[c, core, :, j * block : (j + 1) * block] = part[:, :block]
-            both[c, core, :, mine + j * block : mine + (j + 1) * block] = part[:, block:]
-        send(both.at[c, core], both.at[c, core], pass_send.at[0], pass_recv.at[c], partner, t)
-
-    def product(c, part):
-        left = both[c, :, :, pl.ds(pl.multiple_of(core * mine, mine), mine)].reshape(CORES * piece, mine)
-        right = both[c, :, :, part].reshape(CORES * piece, -1)
+            both[rows_of(c, core), j * block : (j + 1) * block] = part[:, :block]
+            both[rows_of(c, core), mine + j * block : mine + (j + 1) * block] = part[:, block:]
+        for i in range(2):
+            count = sizes[c] // 2
+            shared = both.at[pl.ds(pl.multiple_of(CORES * begins[c] + core * sizes[c] + i * count, 16), count)]
+            send(shared, shared, pass_send.at[0], pass_recv.at[c], partner, t)
+
+    def product(c, part, source=None):
+        first, count = CORES * begins[c], CORES * sizes[c]
+        if source is not None:
+            first, count = first + source * sizes[c], sizes[c]
+        at_rows = slice(first, first + count)
+        left = both[at_rows, pl.ds(pl.multiple_of(core * mine, mine), mine)]
+        right = both[at_rows, part]
         value = lax.dot_general(left, right, (((0,), (0,)), ((), ())), preferred_element_type=F32)
         return value.reshape(ntm, half, right.shape[1])
 
     def partner_rows(c):
-        wait_bytes(both.at[c, 1 - core], pass_recv.at[c])
-
-    lag = 1
-
-    def resample_step(c, carry):
+        wait_bytes(both.at[rows_of(c, 1 - core)], pass_recv.at[c])
+
+    def add(c, source=None):
+        acc[...] += product(c, slice(None), source)
+
+    late = chunks - 1
+    for c in range(late):
         resample(c)
-        return carry
-
-    def add_step(c, carry):
-        partner_rows(c)
-        acc[...] += product(c, slice(None))
-        return carry
-
-    def chunk_step(c, carry):
-        resample(c)
-        return add_step(c - lag, carry)
-
-    lax.fori_loop(0, lag, resample_step, 0)
-
-    own_panels.wait()
-    wait_bytes(panel_all.at[core, pl.ds(0, others), slot], panel_recv.at[0])
-    for d in range(1, nz):
-        peer = lax.rem(zz + d, nz) * CORES + core
-        send(panel_all.at[core, :, slot], panel_all.at[core, :, slot], panel_send.at[1], panel_recv.at[1], peer, t)
-    lax.fori_loop(lag, chunks, chunk_step, 0)
+        if c > 0:
+            partner_rows(c - 1)
+            add(c - 1)
+        if c == 1:
+            own_panels.wait()
+            wait_bytes(panel_all.at[core, pl.ds(0, others), slot], panel_recv.at[0])
+            for d in range(1, nz):
+                peer = lax.rem(zz + d, nz) * CORES + core
+                shared = panel_all.at[core, :, slot]
+                send(shared, shared, panel_send.at[1], panel_recv.at[1], peer, t)
+
+
+    @pl.when(core != 0)
+    def _():
+        resample(late)
+
+    partner_rows(late - 1)
+    add(late - 1)
+
+    @pl.when(core == 0)
+    def _():
+        resample(late)
+        partner_rows(late)
+
+    add(late, 1)
+
+
+    @pl.when(core != 0)
+    def _():
+        partner_rows(late)
+
     parts = [slice(nu - 2 * quarter, nu - quarter), slice(0, nu - 2 * quarter)]
     ahead_part = slice(nu - quarter, nu)
-    partner_rows(chunks - 1)
     def finish(part):
-        total = acc[:, :, part] + product(chunks - 1, part)
+        total = acc[:, :, part] + product(late, part, 0)
         acc[:, :, part] = total
         tm_out[:, :, part] = total.astype(BF16)
 
@@ -302,6 +326,8 @@
     finish(parts[1])
     send_tm(1)
 
+    wait_bytes(panel_all.at[core, :, pl.ds(0, half - own)], panel_recv.at[1])
+    send(panel_all.at[core], panel_all.at[core], panel_send.at[2], panel_recv.at[2], partner, t)
     for h, part in enumerate(parts):
         wait_bytes(tm_in.at[:, :, part], tm_recv.at[h])
         total = acc[pl.ds(t, 1), :, part].reshape(half, part.stop - part.start)
@@ -310,8 +336,6 @@
         z_out[:, :, part] = total.astype(BF16).reshape(nz, own, part.stop - part.start)
         send_line(lambda k: z_out.at[k, :, part], z_in.at[zz, :, part], z_send.at[0], z_recv.at[h])
 
-    wait_bytes(panel_all.at[core, :, pl.ds(0, half - own)], panel_recv.at[1])
-    send(panel_all.at[core], panel_all.at[core], panel_send.at[2], panel_recv.at[2], partner, t)
     wait_bytes(first_in, mix_recv.at[0])
     total = first_in[0].astype(F32)
     for i in range(1, nz):
@@ -322,16 +346,14 @@
         send(first_out.at[peer], second_in.at[i], mix_send.at[1], mix_recv.at[1], space, peer)
     wait_bytes(panel_all.at[1 - core], panel_recv.at[2])
 
-    group = chunks // 2
     table = panel_all[...].reshape(nu, -1)
-    for c in range(0, chunks, group):
-        rows = both[c : c + group, core].reshape(group * piece, nu)
-        value = jnp.dot(rows, table, preferred_element_type=F32)
-        modes_out[c * piece : (c + group) * piece, :] = value.astype(BF16)
+    for c in range(chunks):
+        value = jnp.dot(both[rows_of(c, core), :], table, preferred_element_type=F32)
+        modes_out[begins[c] : begins[c] + sizes[c], :] = value.astype(BF16)
 
     wait_bytes(snap.at[pl.ds(0, others * share), :], row_send.at[0])
     wait_bytes(packed.at[pl.ds(0, others)], table_send.at[0])
-    wait_bytes(both.at[:, 0], pass_send.at[0])
+    wait_bytes(both.at[pl.ds(0, share)], pass_send.at[0])
     wait_bytes(panel_all.at[core, pl.ds(0, others), slot], panel_send.at[0])
     wait_bytes(panel_all.at[core, :, pl.ds(0, half - own)], panel_send.at[1])
     wait_bytes(panel_all.at[core], panel_send.at[2])
@@ -380,14 +402,13 @@
     nmode = panels.shape[1]
     nu, share, nz = block * ntm, rows // ntm, nsp // CORES
     own, half = nu // (ntm * nsp), block // CORES
-    chunks, quarter = CHUNKS, nu // 4
-    piece = share // chunks
+    chunks, quarter = len(SPLIT), nu // 4
     prow = -(-(width_max + 1) // 16) * 16
     vmem = pl.BlockSpec(memory_space=pltpu.VMEM)
     hbm = pl.BlockSpec(memory_space=pltpu.HBM)
     dma = pltpu.SemaphoreType.DMA
     call = pl.pallas_call(
-        functools.partial(kernel, nsp, ntm, chunks, width_max),
+        functools.partial(kernel, nsp, ntm, width_max),
         out_shape=(
             jax.ShapeDtypeStruct((own, nu), F32),
             jax.ShapeDtypeStruct((share, nmode), BF16),
@@ -401,7 +422,7 @@
             pltpu.VMEM((ntm, prow, block), BF16),
             pltpu.VMEM((nu, nu), BF16),
             pltpu.VMEM((share, nu), BF16),
-            pltpu.VMEM((chunks, CORES, piece, nu), BF16),
+            pltpu.VMEM((CORES * share, nu), BF16),
             pltpu.VMEM((ntm, half, nu), F32),
             pltpu.VMEM((ntm, half, nu), BF16),
             pltpu.VMEM((ntm - 1, half, nu - quarter), BF16),
@@ -463,7 +484,7 @@
     def body(snapshots, stencil_starts, stencil_widths, stencil_coeffs, panels):
         rows, block = snapshots.shape
         own = block // nsp
-        fits = block == 128 and own % 16 == 0 and nsp % (CORES * CORES) == 0 and 2 <= ntm <= 4 and ntm & (ntm - 1) == 0 and rows % (64 * ntm) == 0 and block * ntm % 512 == 0
+        fits = block == 128 and own % 16 == 0 and nsp % (CORES * CORES) == 0 and 2 <= ntm <= 4 and ntm & (ntm - 1) == 0 and rows % (256 * ntm) == 0 and block * ntm % 512 == 0
         if fits and 4 * (block * ntm) ** 2 <= 4 * 1024 * 1024:
             return fused(nsp, ntm, snapshots, stencil_starts, stencil_widths, stencil_coeffs, panels)
         return on_device(snapshots, stencil_starts, stencil_widths, stencil_coeffs, panels)

time: 29.7 us -> 29.7 us (level)
  no operation moved by 1% of the time
where the time goes in v3:
time: 29.7 us; the launch traced here: 29.6 us
  Pallas kernels  28.9 us (97%)
  between operations  0.64 us (2%)
    pallas_call x1, Pallas kernels, fused(): call(*(pltpu.with_memory_space_constraint(operand, pltpu.HBM) for operand...  28.1 us
    pallas_call x1, Pallas kernels, fused(): pl.pallas_call(store, out_shape=tuple((jax.ShapeDtypeStruct(value.shape,...  0.81 us

profile of v3, /device:TPU:0, one launch (start us, length us, event | category | flops | bytes accessed | tf_op | source)
XLA Modules:
  0.0 29.6 jit_solution(16402980604476474469)
XLA Ops:
  0.6 28.1 %shard_map.68 = (f32[16,512]{1,0:T(8,128)S(1)}, bf16[1024,256]{1,0:T(8,128)(2,1)S(1)}) custom-call(bf16[4096,128]{1,0:T(8,128)(2,1)} %snap.1, s32[1,128]{1,0:T(1,128)} %bitcast.4, s32[1,128]{1,0:T(1,128)} %bitcast.5, bf16[40,128]{1,0:T(8,128)(2,1)} %bitcast.3, bf16[128,256]{1,0:T(8,128)(2,1)} %panels.1), custom_call_target="tpu_custom_call" | custom-call | tf_op jit(solution)/shard_map/pallas_call | solution.py:460
  28.8 0.8 %shard_map.69 = (f32[16,512]{1,0:T(8,128)}, bf16[1024,256]{1,0:T(8,128)(2,1)}) custom-call(f32[16,512]{1,0:T(8,128)S(1)} %get-tuple-element.4.gram, bf16[1024,256]{1,0:T(8,128)(2,1)S(1)} %get-tuple-element.5.modes), custom_call_target="tpu_custom_call" | custom-call | tf_op jit(solution)/shard_map/pallas_call | solution.py:461

commit v4 on v3

--- a/solution.py
+++ b/solution.py
@@ -293,7 +293,7 @@
     def _():
         partner_rows(late)
 
-    parts = [slice(nu - 2 * quarter, nu - quarter), slice(0, nu - 2 * quarter)]
+    parts = [slice(0, nu - 2 * quarter), slice(nu - 2 * quarter, nu - quarter)]
     ahead_part = slice(nu - quarter, nu)
     def finish(part):
         total = acc[:, :, part] + product(late, part, 0)
@@ -319,11 +319,11 @@
                 def _():
                     send(source, target, send_sem, recv_sem, to_z * CORES + cc, t)
 
+    finish(slice(0, nu - 2 * quarter))
+    send_tm(0)
     finish(slice(nu - 2 * quarter, nu))
     send_line(
         lambda k: tm_out.at[:, pl.ds(k * own, own), ahead_part], first_in.at[zz], mix_send.at[0], mix_recv.at[0])
-    send_tm(0)
-    finish(parts[1])
     send_tm(1)
 
     wait_bytes(panel_all.at[core, :, pl.ds(0, half - own)], panel_recv.at[1])
@@ -365,14 +365,15 @@
     total = first_sum[pl.ds(t, 1)].reshape(own, quarter)
     for i in range(others):
         total = total + second_in[i].astype(F32)
-    sums = [total]
+    ahead = total
+    sums = []
     for h, part in enumerate(parts):
         wait_bytes(z_in.at[:, :, part], z_recv.at[h])
         total = z_in[0, :, part].astype(F32)
         for i in range(1, nz):
             total = total + z_in[i, :, part].astype(F32)
-        sums.insert(0, total)
-    final = jnp.concatenate(sums[:1] + sums[1:], axis=1) * (1.0 / (snap.shape[0] * nsp))
+        sums.append(total)
+    final = jnp.concatenate(sums + [ahead], axis=1) * (1.0 / (snap.shape[0] * nsp))
     low = lax.broadcasted_iota(jnp.int32, (own, block), 1) < half
     for tile in range(ntm):
         at_tile = (tile // 2) * block

time: 29.7 us -> 29.5 us (level)
  no operation moved by 1% of the time
where the time goes in v4:
time: 29.5 us; the launch traced here: 29.4 us
  Pallas kernels  28.8 us (98%)
  between operations  0.64 us (2%)
    pallas_call x1, Pallas kernels, fused(): call(*(pltpu.with_memory_space_constraint(operand, pltpu.HBM) for operand...  27.9 us
    pallas_call x1, Pallas kernels, fused(): pl.pallas_call(store, out_shape=tuple((jax.ShapeDtypeStruct(value.shape,...  0.81 us

profile of v4, /device:TPU:0, one launch (start us, length us, event | category | flops | bytes accessed | tf_op | source)
XLA Modules:
  0.0 29.4 jit_solution(12236675787177593480)
XLA Ops:
  0.6 27.9 %shard_map.68 = (f32[16,512]{1,0:T(8,128)S(1)}, bf16[1024,256]{1,0:T(8,128)(2,1)S(1)}) custom-call(bf16[4096,128]{1,0:T(8,128)(2,1)} %snap.1, s32[1,128]{1,0:T(1,128)} %bitcast.4, s32[1,128]{1,0:T(1,128)} %bitcast.5, bf16[40,128]{1,0:T(8,128)(2,1)} %bitcast.3, bf16[128,256]{1,0:T(8,128)(2,1)} %panels.1), custom_call_target="tpu_custom_call" | custom-call | tf_op jit(solution)/shard_map/pallas_call | solution.py:461
  28.6 0.8 %shard_map.69 = (f32[16,512]{1,0:T(8,128)}, bf16[1024,256]{1,0:T(8,128)(2,1)}) custom-call(f32[16,512]{1,0:T(8,128)S(1)} %get-tuple-element.4.gram, bf16[1024,256]{1,0:T(8,128)(2,1)S(1)} %get-tuple-element.5.modes), custom_call_target="tpu_custom_call" | custom-call | tf_op jit(solution)/shard_map/pallas_call | solution.py:462
